TPU v7x, 32 devices: a whole 2x2x4 slice. The times are simulated.
32 devices in a mesh: member: 2 (over y), vec: 4 (over x, core), band: 4 (over z).
Axes of the slice: x: 2, y: 2, z: 4, core: 2. Of those that a mesh axis runs over, the one named last changes fastest.
Arguments:
- vectors: float32 [32, 3, 16, 1440], P(('member', 'vec'), None, 'band'), parts along dimension 0, may hold values from -6 to 6
- flow: float32 [4, 16, 1440], P(None, 'band'), may hold values from -1 to 1
- band_cut: int32 [16], replicated, may hold values from 2 to 127
- order: int32 [4], replicated, may hold values from 0 to 3, each once
Outputs:
- basis: float32 [32, 3, 16, 1440], P(('member', 'vec'), None, 'band'), parts along dimension 0
- growth: float32 [32], P(('member', 'vec')), parts along dimension 0
There are 2 independent parts, one for each index of `member`. A program takes and returns all parts, laid end to end along the dimension named above; an argument that names none is the same for every part. Nothing has to cross between parts.
Inputs may be any that keep to these rules, and one draw needn't show every extreme that they name: `order`: each block number appears once.
All inputs are finite; a program needn't handle non-finite values.
Results may differ from a plain program's by a relative error of at most 0.0001.
Values sent between devices are 32-bit elements; how exact they have to be, the bound alone decides.
A program may use at most 64 MiB of HBM per device.

v0:
```python
import math
import jax
import jax.numpy as jnp
from jax import lax
from jax.sharding import PartitionSpec as P

KMAX = 128
CAP_DEV = 2
step_dt = 0.4
half_dt = 0.2
sixth_dt = 0.4 / 6.0


def extended(block, sides, width):
    for axis, dim in sides:
        count = lax.axis_size(axis)
        forward = [(i, i + 1) for i in range(count - 1)]
        backward = [(target, source) for source, target in forward]
        low = lax.ppermute(
            lax.slice_in_dim(block, block.shape[dim] - width, None, axis=dim), axis, forward
        )
        high = lax.ppermute(lax.slice_in_dim(block, 0, width, axis=dim), axis, backward)
        block = jnp.concatenate([low, block, high], axis=dim)
    return block


def broadcast(value, axis, source):
    kept = jnp.where(lax.axis_index(axis) == source, value, 0).astype(value.dtype)
    return lax.psum(kept, axis)


def tendency(z, coef):
    inner = z[:, :, 1:-1]
    dx = 0.5 * (jnp.roll(inner, -1, 3) - jnp.roll(inner, 1, 3))
    dy = 0.5 * (z[:, :, 2:] - z[:, :, :-2])
    speed_x = coef[0]
    speed_y = coef[1]
    depth = 1.0 + 0.5 * coef[2]
    rotation = 0.5 * coef[3]
    advect = -(speed_x * dx + speed_y * dy)
    t_height = advect[:, 0] - depth * (dx[:, 1] + dy[:, 2])
    t_zonal = advect[:, 1] - dx[:, 0] + rotation * inner[:, 2]
    t_merid = advect[:, 2] - dy[:, 0] - rotation * inner[:, 1]
    return jnp.stack([t_height, t_zonal, t_merid], 1)


def with_rows(state):
    return extended(state, (("band", 2),), 1)


def step_near(state, flow):
    k_one = tendency(with_rows(state), flow)
    k_two = tendency(with_rows(state + half_dt * k_one), flow)
    k_three = tendency(with_rows(state + half_dt * k_two), flow)
    k_four = tendency(with_rows(state + step_dt * k_three), flow)
    return state + sixth_dt * (k_one + 2.0 * k_two + 2.0 * k_three + k_four)


def mode_table(nlon, kmax):
    points = jnp.arange(nlon, dtype=jnp.int32)
    waves = jnp.arange(kmax, dtype=jnp.int32)
    phase = (waves[:, None] * points[None, :] % nlon).astype(jnp.float32) * (2.0 * math.pi / nlon)
    scale = jnp.where(waves == 0, math.sqrt(1.0 / nlon), math.sqrt(2.0 / nlon)).astype(jnp.float32)
    cosines = jnp.cos(phase) * scale[:, None]
    sines = jnp.sin(phase) * math.sqrt(2.0 / nlon)
    return jnp.concatenate([cosines, sines], 0)


def project(rows, cutoff, table, kmax):
    waves = jnp.arange(kmax, dtype=jnp.int32)
    wave_both = jnp.concatenate([waves, waves], 0)
    keep = (wave_both <= cutoff[..., None]).astype(jnp.float32)
    coeffs = jnp.einsum("...l,kl->...k", rows, table, precision=lax.Precision.HIGHEST)
    return jnp.einsum("...k,kl->...l", coeffs * keep, table, precision=lax.Precision.HIGHEST)


def polar_filter(state, band_cut, table):
    nband = lax.axis_size("band")
    me_band = lax.axis_index("band")
    lat_dev = state.shape[2]
    cap_rows = CAP_DEV * lat_dev
    north = me_band < CAP_DEV
    south = me_band >= nband - CAP_DEV
    start = jnp.where(north, me_band * lat_dev, cap_rows + (me_band - nband + CAP_DEV) * lat_dev)
    start = jnp.clip(start, 0, 2 * cap_rows - lat_dev)
    cutoff = lax.dynamic_slice_in_dim(band_cut, start, lat_dev)
    return lax.cond(
        north | south, lambda value: project(value, cutoff, table, KMAX), lambda value: value, state
    )


def on_device(vectors, flow, band_cut, order):
    state = vectors
    nband = lax.axis_size("band")
    lat_dev = state.shape[2]
    table = mode_table(state.shape[3], KMAX)
    for inner_step in range(2):
        state = step_near(state, flow)
    state = polar_filter(state, band_cut, table)
    nblocks = lax.axis_size("vec")
    me_vec = lax.axis_index("vec")
    vec_dev = state.shape[0]
    total = float(3 * nband * lat_dev * state.shape[3])
    flat = state.reshape(vec_dev, -1)
    numbers = jnp.arange(nblocks, dtype=jnp.int32)
    position = jnp.sum(jnp.where(order == me_vec, numbers, 0))
    growth = jnp.zeros((vec_dev,), jnp.float32)
    for turn in range(nblocks):
        panel = broadcast(flat, "vec", order[turn])
        gram = lax.psum(jnp.dot(panel, panel.T, precision=lax.Precision.HIGHEST), "band") / total
        lower = jnp.linalg.cholesky(gram)
        ortho = jax.scipy.linalg.solve_triangular(lower, panel, lower=True)
        coef = lax.psum(jnp.dot(flat, ortho.T, precision=lax.Precision.HIGHEST), "band") / total
        update = flat - jnp.dot(coef, ortho, precision=lax.Precision.HIGHEST)
        flat = jnp.where(position > turn, update, jnp.where(position == turn, ortho, flat))
        growth = jnp.where(position == turn, jnp.log(jnp.diagonal(lower)), growth)
    return (flat.reshape(state.shape), growth)


def solution(mesh):
    in_specs = (P(("member", "vec"), None, "band", None), P(None, "band", None), P(), P())
    out_specs = (P(("member", "vec"), None, "band", None), P(("member", "vec")))
    return jax.shard_map(
        on_device, mesh=mesh, in_specs=in_specs, out_specs=out_specs, check_vma=False
    )
```

profile of v0, /device:TPU:0, one launch (start us, length us, event | category | flops | bytes accessed | tf_op | source)
XLA Modules:
  0.0 348.0 jit_solution(16133141258340314673)
XLA Ops:
  7.2 1.9 fusion.110
  9.1 1.3 collective-permute-start
  10.4 5.6 %collective-permute-start.1 = (f32[4,3,1,1440]{3,2,1,0:T(1,128)}, f32[4,3,1,1440]{3,2,1,0:T(1,128)S(1)}, u32[]{:S(2)}, u32[]{:S(2)}) collective-permute-start(f32[4,3,1,1440]{3,2,1,0:T(1,128)} %get-tuple-element.172), channel_id=1, source_target_pairs={{0,1},{1,2},{2,3},{4,5},{5,6},{6,7},{8,9},{9,10},{10,11},{12,13},{... | collective-permute-start | bytes 207368 | tf_op jit(solution)/shard_map/ppermute | solution.py:19
  16.0 2.0 fusion.108
  18.1 3.1 sine_multiply_fusion
  21.9 0.7 fusion.111
  23.9 1.6 broadcast_multiply_fusion.15
  26.0 1.3 collective-permute-start.2
  27.3 4.6 %collective-permute-start.3 = (f32[4,3,1,1440]{3,2,1,0:T(1,128)S(1)}, f32[4,3,1,1440]{3,2,1,0:T(1,128)S(1)}, u32[]{:S(2)}, u32[]{:S(2)}) collective-permute-start(f32[4,3,1,1440]{3,2,1,0:T(1,128)S(1)} %get-tuple-element.166), channel_id=1, source_target_pairs={{0,1},{1,2},{2,3},{4,5},{5,6},{6,7},{8,9},{9,10},{10,11},{12,13},{... | collective-permute-start | bytes 207368 | tf_op jit(solution)/shard_map/ppermute | solution.py:19
  32.3 1.6 collective-permute-done.3
  34.9 1.3 collective-permute-start.4
  36.2 4.9 %collective-permute-start.5 = (f32[4,3,1,1440]{3,2,1,0:T(1,128)S(1)}, f32[4,3,1,1440]{3,2,1,0:T(1,128)S(1)}, u32[]{:S(2)}, u32[]{:S(2)}) collective-permute-start(f32[4,3,1,1440]{3,2,1,0:T(1,128)S(1)} %get-tuple-element.160), channel_id=1, source_target_pairs={{0,1},{1,2},{2,3},{4,5},{5,6},{6,7},{8,9},{9,10},{10,11},{12,13},{... | collective-permute-start | bytes 207368 | tf_op jit(solution)/shard_map/ppermute | solution.py:19
  41.5 1.6 collective-permute-done.5
  44.2 1.3 collective-permute-start.6
  45.5 4.9 %collective-permute-start.7 = (f32[4,3,1,1440]{3,2,1,0:T(1,128)S(1)}, f32[4,3,1,1440]{3,2,1,0:T(1,128)S(1)}, u32[]{:S(2)}, u32[]{:S(2)}) collective-permute-start(f32[4,3,1,1440]{3,2,1,0:T(1,128)S(1)} %get-tuple-element.154), channel_id=1, source_target_pairs={{0,1},{1,2},{2,3},{4,5},{5,6},{6,7},{8,9},{9,10},{10,11},{12,13},{... | collective-permute-start | bytes 207368 | tf_op jit(solution)/shard_map/ppermute | solution.py:19
  50.8 1.6 collective-permute-done.7
  53.6 1.3 collective-permute-start.8
  54.9 4.9 %collective-permute-start.9 = (f32[4,3,1,1440]{3,2,1,0:T(1,128)S(1)}, f32[4,3,1,1440]{3,2,1,0:T(1,128)S(1)}, u32[]{:S(2)}, u32[]{:S(2)}) collective-permute-start(f32[4,3,1,1440]{3,2,1,0:T(1,128)S(1)} %get-tuple-element.148), channel_id=1, source_target_pairs={{0,1},{1,2},{2,3},{4,5},{5,6},{6,7},{8,9},{9,10},{10,11},{12,13},{... | collective-permute-start | bytes 207368 | tf_op jit(solution)/shard_map/ppermute | solution.py:19
  60.2 1.6 collective-permute-done.9
  63.1 1.3 collective-permute-start.10
  64.4 5.1 %collective-permute-start.11 = (f32[4,3,1,1440]{3,2,1,0:T(1,128)S(1)}, f32[4,3,1,1440]{3,2,1,0:T(1,128)S(1)}, u32[]{:S(2)}, u32[]{:S(2)}) collective-permute-start(f32[4,3,1,1440]{3,2,1,0:T(1,128)S(1)} %get-tuple-element.142), channel_id=1, source_target_pairs={{0,1},{1,2},{2,3},{4,5},{5,6},{6,7},{8,9},{9,10},{10,11},{12,13},{... | collective-permute-start | bytes 207368 | tf_op jit(solution)/shard_map/ppermute | solution.py:19
  69.7 1.6 collective-permute-done.11
  72.5 1.3 collective-permute-start.12
  73.8 4.9 %collective-permute-start.13 = (f32[4,3,1,1440]{3,2,1,0:T(1,128)S(1)}, f32[4,3,1,1440]{3,2,1,0:T(1,128)S(1)}, u32[]{:S(2)}, u32[]{:S(2)}) collective-permute-start(f32[4,3,1,1440]{3,2,1,0:T(1,128)S(1)} %get-tuple-element.136), channel_id=1, source_target_pairs={{0,1},{1,2},{2,3},{4,5},{5,6},{6,7},{8,9},{9,10},{10,11},{12,13},{... | collective-permute-start | bytes 207368 | tf_op jit(solution)/shard_map/ppermute | solution.py:19
  79.1 1.6 collective-permute-done.13
  82.0 1.3 collective-permute-start.14
  83.3 4.9 %collective-permute-start.15 = (f32[4,3,1,1440]{3,2,1,0:T(1,128)S(1)}, f32[4,3,1,1440]{3,2,1,0:T(1,128)S(1)}, u32[]{:S(2)}, u32[]{:S(2)}) collective-permute-start(f32[4,3,1,1440]{3,2,1,0:T(1,128)S(1)} %get-tuple-element.130), channel_id=1, source_target_pairs={{0,1},{1,2},{2,3},{4,5},{5,6},{6,7},{8,9},{9,10},{10,11},{12,13},{... | collective-permute-start | bytes 207368 | tf_op jit(solution)/shard_map/ppermute | solution.py:19
  88.6 1.6 collective-permute-done.15
  91.4 2.6 conditional.1
  91.6 1.0 fusion.4
  92.7 1.4 fusion
  94.4 0.8 broadcast_select_fusion.3
  95.3 0.7 fusion.81
  97.8 32.7 %all-reduce.5.cloned.1.call-done = f32[4,17280]{1,0:T(4,128)} async-done(((f32[4,17280]{1,0:T(4,128)}), f32[4,17280]{1,0:T(4,128)}) %all-reduce.5.cloned.1.call-update) | async-done | bytes 276496 | tf_op jit(solution)/shard_map/psum | solution.py:29
  130.6 2.3 fusion.112
  132.9 11.7 %psum.85 = f32[4,4]{0,1:T(4,128)S(1)} all-reduce(f32[4,4]{0,1:T(4,128)S(1)} %fusion.112), channel_id=1, replica_groups=mesh['member'=2,'vec'=4,'band'=4] {'band'}, use_global_device_ids=true, to_apply=%region_4.5 | all-reduce | flops 16 | bytes 128 | tf_op jit(solution)/shard_map/psum | solution.py:110
  146.7 1.7 fusion.66
  148.4 1.3 fusion.113
  149.7 8.4 %psum.86 = f32[4,4]{0,1:T(4,128)S(1)} all-reduce(f32[4,4]{0,1:T(4,128)S(1)} %fusion.113), channel_id=1, replica_groups=mesh['member'=2,'vec'=4,'band'=4] {'band'}, use_global_device_ids=true, to_apply=%region_7.10 | all-reduce | flops 16 | bytes 128 | tf_op jit(solution)/shard_map/psum | solution.py:113
  158.1 1.5 broadcast_select_fusion.2
  161.5 29.0 %all-reduce.7.cloned.1.call-done = f32[4,17280]{1,0:T(4,128)} async-done(((f32[4,17280]{1,0:T(4,128)}), f32[4,17280]{1,0:T(4,128)}) %all-reduce.7.cloned.1.call-update) | async-done | bytes 276496 | tf_op jit(solution)/shard_map/psum | solution.py:29
  190.6 2.3 fusion.114
  192.9 11.9 %psum.88 = f32[4,4]{0,1:T(4,128)S(1)} all-reduce(f32[4,4]{0,1:T(4,128)S(1)} %fusion.114), channel_id=1, replica_groups=mesh['member'=2,'vec'=4,'band'=4] {'band'}, use_global_device_ids=true, to_apply=%region_9.12 | all-reduce | flops 16 | bytes 128 | tf_op jit(solution)/shard_map/psum | solution.py:110
  206.0 0.6 select_bitcast_fusion.2
  207.0 1.7 fusion.64
  208.7 1.3 fusion.115
  210.0 8.4 %psum.89 = f32[4,4]{0,1:T(4,128)S(1)} all-reduce(f32[4,4]{0,1:T(4,128)S(1)} %fusion.115), channel_id=1, replica_groups=mesh['member'=2,'vec'=4,'band'=4] {'band'}, use_global_device_ids=true, to_apply=%region_10.13 | all-reduce | flops 16 | bytes 128 | tf_op jit(solution)/shard_map/psum | solution.py:113
  218.3 1.5 broadcast_select_fusion.1
  221.8 29.0 %all-reduce.9.cloned.1.call-done = f32[4,17280]{1,0:T(4,128)} async-done(((f32[4,17280]{1,0:T(4,128)}), f32[4,17280]{1,0:T(4,128)}) %all-reduce.9.cloned.1.call-update) | async-done | bytes 276496 | tf_op jit(solution)/shard_map/psum | solution.py:29
  250.8 2.3 fusion.116
  253.2 11.7 %psum.91 = f32[4,4]{0,1:T(4,128)S(1)} all-reduce(f32[4,4]{0,1:T(4,128)S(1)} %fusion.116), channel_id=1, replica_groups=mesh['member'=2,'vec'=4,'band'=4] {'band'}, use_global_device_ids=true, to_apply=%region_12.15 | all-reduce | flops 16 | bytes 128 | tf_op jit(solution)/shard_map/psum | solution.py:110
  267.0 1.7 fusion.62
  268.7 1.3 fusion.117
  270.0 8.4 %psum.92 = f32[4,4]{0,1:T(4,128)S(1)} all-reduce(f32[4,4]{0,1:T(4,128)S(1)} %fusion.117), channel_id=1, replica_groups=mesh['member'=2,'vec'=4,'band'=4] {'band'}, use_global_device_ids=true, to_apply=%region_13.16 | all-reduce | flops 16 | bytes 128 | tf_op jit(solution)/shard_map/psum | solution.py:113
  278.4 1.5 broadcast_select_fusion
  283.1 27.8 %all-reduce.11.cloned.1.call-done = f32[4,17280]{1,0:T(4,128)} async-done(((f32[4,17280]{1,0:T(4,128)}), f32[4,17280]{1,0:T(4,128)}) %all-reduce.11.cloned.1.call-update) | async-done | bytes 276496 | tf_op jit(solution)/shard_map/psum | solution.py:29
  310.9 2.3 fusion.118
  313.3 11.7 %psum.94 = f32[4,4]{0,1:T(4,128)S(1)} all-reduce(f32[4,4]{0,1:T(4,128)S(1)} %fusion.118), channel_id=1, replica_groups=mesh['member'=2,'vec'=4,'band'=4] {'band'}, use_global_device_ids=true, to_apply=%region_15.18 | all-reduce | flops 16 | bytes 128 | tf_op jit(solution)/shard_map/psum | solution.py:110
  326.1 0.6 select_bitcast_fusion
  327.7 1.7 fusion.60
  329.4 1.3 fusion.119
  330.7 8.4 %psum.95 = f32[4,4]{0,1:T(4,128)S(1)} all-reduce(f32[4,4]{0,1:T(4,128)S(1)} %fusion.119), channel_id=1, replica_groups=mesh['member'=2,'vec'=4,'band'=4] {'band'}, use_global_device_ids=true, to_apply=%region_16.19 | all-reduce | flops 16 | bytes 128 | tf_op jit(solution)/shard_map/psum | solution.py:113
  339.1 0.8 fusion.7
  339.9 1.1 reshape.65
  (118 shorter events, 24.0 us)
Async XLA Ops:
  7.2 10.8 %copy-start = (f32[4,3,4,1440]{3,2,1,0:T(4,128)S(1)}, f32[4,3,4,1440]{3,2,1,0:T(4,128)}, u32[]{:S(2)}) copy-start(f32[4,3,4,1440]{3,2,1,0:T(4,128)} %param.9) | copy-start | bytes 829444
  7.2 10.9 %copy-start.1 = (f32[4,4,1440]{2,1,0:T(4,128)S(1)}, f32[4,4,1440]{2,1,0:T(4,128)}, u32[]{:S(2)}) copy-start(f32[4,4,1440]{2,1,0:T(4,128)} %param.10) | copy-start | bytes 276484
  7.2 123.4 %all-reduce.5.cloned.1.call-start = ((), (), s32[]{:S(2)}) async-start(), calls=%async_computation | async-start | bytes 552960 | tf_op jit(solution)/shard_map/psum | solution.py:29
  9.1 14.1 %collective-permute-start = (f32[4,3,1,1440]{3,2,1,0:T(1,128)}, f32[4,3,1,1440]{3,2,1,0:T(1,128)S(1)}, u32[]{:S(2)}, u32[]{:S(2)}) collective-permute-start(f32[4,3,1,1440]{3,2,1,0:T(1,128)} %get-tuple-element.171), channel_id=1, source_target_pairs={{1,0},{2,1},{3,2},{5,4},{6,5},{7,6},{9,8},{10,9},{11,10},{13,12},{... | collective-permute-start | bytes 207368 | tf_op jit(solution)/shard_map/ppermute | solution.py:22
  10.4 12.8 %collective-permute-start.1 = (f32[4,3,1,1440]{3,2,1,0:T(1,128)}, f32[4,3,1,1440]{3,2,1,0:T(1,128)S(1)}, u32[]{:S(2)}, u32[]{:S(2)}) collective-permute-start(f32[4,3,1,1440]{3,2,1,0:T(1,128)} %get-tuple-element.172), channel_id=1, source_target_pairs={{0,1},{1,2},{2,3},{4,5},{5,6},{6,7},{8,9},{9,10},{10,11},{12,13},{... | collective-permute-start | bytes 207368 | tf_op jit(solution)/shard_map/ppermute | solution.py:19
  21.2 0.7 copy-start.4
  23.2 0.6 copy-start.2
  23.2 0.6 copy-start.3
  26.0 6.2 %collective-permute-start.2 = (f32[4,3,1,1440]{3,2,1,0:T(1,128)S(1)}, f32[4,3,1,1440]{3,2,1,0:T(1,128)S(1)}, u32[]{:S(2)}, u32[]{:S(2)}) collective-permute-start(f32[4,3,1,1440]{3,2,1,0:T(1,128)S(1)} %get-tuple-element.165), channel_id=1, source_target_pairs={{1,0},{2,1},{3,2},{5,4},{6,5},{7,6},{9,8},{10,9},{11,10},{13,12},{... | collective-permute-start | bytes 207368 | tf_op jit(solution)/shard_map/ppermute | solution.py:22
  27.3 6.5 %collective-permute-start.3 = (f32[4,3,1,1440]{3,2,1,0:T(1,128)S(1)}, f32[4,3,1,1440]{3,2,1,0:T(1,128)S(1)}, u32[]{:S(2)}, u32[]{:S(2)}) collective-permute-start(f32[4,3,1,1440]{3,2,1,0:T(1,128)S(1)} %get-tuple-element.166), channel_id=1, source_target_pairs={{0,1},{1,2},{2,3},{4,5},{5,6},{6,7},{8,9},{9,10},{10,11},{12,13},{... | collective-permute-start | bytes 207368 | tf_op jit(solution)/shard_map/ppermute | solution.py:19
  34.9 6.6 %collective-permute-start.4 = (f32[4,3,1,1440]{3,2,1,0:T(1,128)S(1)}, f32[4,3,1,1440]{3,2,1,0:T(1,128)S(1)}, u32[]{:S(2)}, u32[]{:S(2)}) collective-permute-start(f32[4,3,1,1440]{3,2,1,0:T(1,128)S(1)} %get-tuple-element.159), channel_id=1, source_target_pairs={{1,0},{2,1},{3,2},{5,4},{6,5},{7,6},{9,8},{10,9},{11,10},{13,12},{... | collective-permute-start | bytes 207368 | tf_op jit(solution)/shard_map/ppermute | solution.py:22
  36.2 6.9 %collective-permute-start.5 = (f32[4,3,1,1440]{3,2,1,0:T(1,128)S(1)}, f32[4,3,1,1440]{3,2,1,0:T(1,128)S(1)}, u32[]{:S(2)}, u32[]{:S(2)}) collective-permute-start(f32[4,3,1,1440]{3,2,1,0:T(1,128)S(1)} %get-tuple-element.160), channel_id=1, source_target_pairs={{0,1},{1,2},{2,3},{4,5},{5,6},{6,7},{8,9},{9,10},{10,11},{12,13},{... | collective-permute-start | bytes 207368 | tf_op jit(solution)/shard_map/ppermute | solution.py:19
  44.2 6.6 %collective-permute-start.6 = (f32[4,3,1,1440]{3,2,1,0:T(1,128)S(1)}, f32[4,3,1,1440]{3,2,1,0:T(1,128)S(1)}, u32[]{:S(2)}, u32[]{:S(2)}) collective-permute-start(f32[4,3,1,1440]{3,2,1,0:T(1,128)S(1)} %get-tuple-element.153), channel_id=1, source_target_pairs={{1,0},{2,1},{3,2},{5,4},{6,5},{7,6},{9,8},{10,9},{11,10},{13,12},{... | collective-permute-start | bytes 207368 | tf_op jit(solution)/shard_map/ppermute | solution.py:22
  45.5 6.9 %collective-permute-start.7 = (f32[4,3,1,1440]{3,2,1,0:T(1,128)S(1)}, f32[4,3,1,1440]{3,2,1,0:T(1,128)S(1)}, u32[]{:S(2)}, u32[]{:S(2)}) collective-permute-start(f32[4,3,1,1440]{3,2,1,0:T(1,128)S(1)} %get-tuple-element.154), channel_id=1, source_target_pairs={{0,1},{1,2},{2,3},{4,5},{5,6},{6,7},{8,9},{9,10},{10,11},{12,13},{... | collective-permute-start | bytes 207368 | tf_op jit(solution)/shard_map/ppermute | solution.py:19
  53.6 6.6 %collective-permute-start.8 = (f32[4,3,1,1440]{3,2,1,0:T(1,128)S(1)}, f32[4,3,1,1440]{3,2,1,0:T(1,128)S(1)}, u32[]{:S(2)}, u32[]{:S(2)}) collective-permute-start(f32[4,3,1,1440]{3,2,1,0:T(1,128)S(1)} %get-tuple-element.147), channel_id=1, source_target_pairs={{1,0},{2,1},{3,2},{5,4},{6,5},{7,6},{9,8},{10,9},{11,10},{13,12},{... | collective-permute-start | bytes 207368 | tf_op jit(solution)/shard_map/ppermute | solution.py:22
  54.9 6.9 %collective-permute-start.9 = (f32[4,3,1,1440]{3,2,1,0:T(1,128)S(1)}, f32[4,3,1,1440]{3,2,1,0:T(1,128)S(1)}, u32[]{:S(2)}, u32[]{:S(2)}) collective-permute-start(f32[4,3,1,1440]{3,2,1,0:T(1,128)S(1)} %get-tuple-element.148), channel_id=1, source_target_pairs={{0,1},{1,2},{2,3},{4,5},{5,6},{6,7},{8,9},{9,10},{10,11},{12,13},{... | collective-permute-start | bytes 207368 | tf_op jit(solution)/shard_map/ppermute | solution.py:19
  63.1 6.6 %collective-permute-start.10 = (f32[4,3,1,1440]{3,2,1,0:T(1,128)S(1)}, f32[4,3,1,1440]{3,2,1,0:T(1,128)S(1)}, u32[]{:S(2)}, u32[]{:S(2)}) collective-permute-start(f32[4,3,1,1440]{3,2,1,0:T(1,128)S(1)} %get-tuple-element.141), channel_id=1, source_target_pairs={{1,0},{2,1},{3,2},{5,4},{6,5},{7,6},{9,8},{10,9},{11,10},{13,12},{... | collective-permute-start | bytes 207368 | tf_op jit(solution)/shard_map/ppermute | solution.py:22
  64.4 6.9 %collective-permute-start.11 = (f32[4,3,1,1440]{3,2,1,0:T(1,128)S(1)}, f32[4,3,1,1440]{3,2,1,0:T(1,128)S(1)}, u32[]{:S(2)}, u32[]{:S(2)}) collective-permute-start(f32[4,3,1,1440]{3,2,1,0:T(1,128)S(1)} %get-tuple-element.142), channel_id=1, source_target_pairs={{0,1},{1,2},{2,3},{4,5},{5,6},{6,7},{8,9},{9,10},{10,11},{12,13},{... | collective-permute-start | bytes 207368 | tf_op jit(solution)/shard_map/ppermute | solution.py:19
  72.5 6.6 %collective-permute-start.12 = (f32[4,3,1,1440]{3,2,1,0:T(1,128)S(1)}, f32[4,3,1,1440]{3,2,1,0:T(1,128)S(1)}, u32[]{:S(2)}, u32[]{:S(2)}) collective-permute-start(f32[4,3,1,1440]{3,2,1,0:T(1,128)S(1)} %get-tuple-element.135), channel_id=1, source_target_pairs={{1,0},{2,1},{3,2},{5,4},{6,5},{7,6},{9,8},{10,9},{11,10},{13,12},{... | collective-permute-start | bytes 207368 | tf_op jit(solution)/shard_map/ppermute | solution.py:22
  73.8 6.9 %collective-permute-start.13 = (f32[4,3,1,1440]{3,2,1,0:T(1,128)S(1)}, f32[4,3,1,1440]{3,2,1,0:T(1,128)S(1)}, u32[]{:S(2)}, u32[]{:S(2)}) collective-permute-start(f32[4,3,1,1440]{3,2,1,0:T(1,128)S(1)} %get-tuple-element.136), channel_id=1, source_target_pairs={{0,1},{1,2},{2,3},{4,5},{5,6},{6,7},{8,9},{9,10},{10,11},{12,13},{... | collective-permute-start | bytes 207368 | tf_op jit(solution)/shard_map/ppermute | solution.py:19
  82.0 6.6 %collective-permute-start.14 = (f32[4,3,1,1440]{3,2,1,0:T(1,128)S(1)}, f32[4,3,1,1440]{3,2,1,0:T(1,128)S(1)}, u32[]{:S(2)}, u32[]{:S(2)}) collective-permute-start(f32[4,3,1,1440]{3,2,1,0:T(1,128)S(1)} %get-tuple-element.129), channel_id=1, source_target_pairs={{1,0},{2,1},{3,2},{5,4},{6,5},{7,6},{9,8},{10,9},{11,10},{13,12},{... | collective-permute-start | bytes 207368 | tf_op jit(solution)/shard_map/ppermute | solution.py:22
  83.3 6.9 %collective-permute-start.15 = (f32[4,3,1,1440]{3,2,1,0:T(1,128)S(1)}, f32[4,3,1,1440]{3,2,1,0:T(1,128)S(1)}, u32[]{:S(2)}, u32[]{:S(2)}) collective-permute-start(f32[4,3,1,1440]{3,2,1,0:T(1,128)S(1)} %get-tuple-element.130), channel_id=1, source_target_pairs={{0,1},{1,2},{2,3},{4,5},{5,6},{6,7},{8,9},{9,10},{10,11},{12,13},{... | collective-permute-start | bytes 207368 | tf_op jit(solution)/shard_map/ppermute | solution.py:19
  90.8 0.7 copy-start.5
  95.2 95.4 %all-reduce.7.cloned.1.call-start = ((), (), s32[]{:S(2)}) async-start(), calls=%async_computation.1 | async-start | bytes 552960 | tf_op jit(solution)/shard_map/psum | solution.py:29
  159.6 91.2 %all-reduce.9.cloned.1.call-start = ((), (), s32[]{:S(2)}) async-start(), calls=%async_computation.2 | async-start | bytes 552960 | tf_op jit(solution)/shard_map/psum | solution.py:29
  219.9 91.0 %all-reduce.11.cloned.1.call-start = ((), (), s32[]{:S(2)}) async-start(), calls=%async_computation.3 | async-start | bytes 552960 | tf_op jit(solution)/shard_map/psum | solution.py:29
Sparse Core Ops, SparseCore 0:
  95.4 35.1 all-reduce.4
  159.7 30.8 all-reduce.6
  220.0 30.8 all-reduce.8
  280.1 30.8 all-reduce.10
where the time goes:
time: 349 us; the launch traced here: 348 us
  waiting for transfers between devices  132 us (38%)
  blocking collectives  80.3 us (23%)
  starting transfers between devices  50.2 us (14%)
  matrix products  29.2 us (8%)
  between operations  21.9 us (6%)
  other arithmetic  21.5 us (6%)
  local copies, waits for them, and re-layouts  13.3 us (4%)
    psum x4, waiting for transfers between devices, broadcast(): return lax.psum(kept, axis)  119 us
    psum x4, blocking collectives, on_device(): lax.psum(jnp.dot(panel, panel.T, precision=lax.Precision.HIGHEST), 'band')  46.9 us
    ppermute x8, starting transfers between devices, extended(): lax.ppermute(lax.slice_in_dim(block, block.shape[dim] - width, None, axis...  39.7 us
    psum x4, blocking collectives, on_device(): lax.psum(jnp.dot(flat, ortho.T, precision=lax.Precision.HIGHEST), 'band')  33.4 us
    ppermute x8, waiting for transfers between devices, extended(): lax.ppermute(lax.slice_in_dim(block, block.shape[dim] - width, None, axis...  11 us
    ppermute x8, starting transfers between devices, extended(): lax.ppermute(lax.slice_in_dim(block, 0, width, axis=dim), axis, backward)  10.3 us
    dot_general x4, matrix products, on_device(): jnp.dot(panel, panel.T, precision=lax.Precision.HIGHEST)  9.4 us
  transfers between devices with their start and end apart: 20, of which 18 were waited for; matrix products, arithmetic and copies ran while one was open for 3% of the time, Pallas kernels for 0%

commit v1 on v0

--- a/solution.py
+++ b/solution.py
@@ -9,6 +9,12 @@
 step_dt = 0.4
 half_dt = 0.2
 sixth_dt = 0.4 / 6.0
+
+
+def gather_and_add(x, axis):
+    parts = lax.all_gather(x, axis, axis=0, tiled=False)
+    summed = parts.sum(axis=0)
+    return summed
 
 
 def extended(block, sides, width):
@@ -26,7 +32,7 @@
 
 def broadcast(value, axis, source):
     kept = jnp.where(lax.axis_index(axis) == source, value, 0).astype(value.dtype)
-    return lax.psum(kept, axis)
+    return gather_and_add(kept, axis)
 
 
 def tendency(z, coef):

time: 349 us -> 288 us (0.83)
  waiting for transfers between devices: 132 us -> 71.7 us
  matrix products: 29.2 us -> 18.9 us
  other arithmetic: 21.5 us -> 29.1 us
    psum x4 -> x0, waiting for transfers between devices: 119 us -> none  [broadcast(): return lax.psum(kept, axis)]
    all_gather x0 -> x4, waiting for transfers between devices: none -> 58.6 us  [gather_and_add(): parts = lax.all_gather(x, axis, axis=0, tiled=False)]
    reduce_sum x0 -> x4, other arithmetic: none -> 6.01 us  [gather_and_add(): summed = parts.sum(axis=0)]
    dot_general x4, matrix products: 9.4 us -> 5.12 us  [on_device(): jnp.dot(panel, panel.T, precision=lax.Precision.HIGHEST)]
    another operation x4, matrix products: 6.71 us -> 2.91 us  [on_device(): ortho = jax.scipy.linalg.solve_triangular(lower, panel, lower=True)]
where the time goes in v1:
time: 288 us; the launch traced here: 287 us
  blocking collectives  80.4 us (28%)
  waiting for transfers between devices  71.7 us (25%)
  starting transfers between devices  50.2 us (17%)
  other arithmetic  29.1 us (10%)
  between operations  21.8 us (8%)
  matrix products  18.9 us (7%)
  local copies, waits for them, and re-layouts  14.4 us (5%)
    all_gather x4, waiting for transfers between devices, gather_and_add(): parts = lax.all_gather(x, axis, axis=0, tiled=False)  58.6 us
    psum x4, blocking collectives, on_device(): lax.psum(jnp.dot(panel, panel.T, precision=lax.Precision.HIGHEST), 'band')  46.9 us
    ppermute x8, starting transfers between devices, extended(): lax.ppermute(lax.slice_in_dim(block, block.shape[dim] - width, None, axis...  39.7 us
    psum x4, blocking collectives, on_device(): lax.psum(jnp.dot(flat, ortho.T, precision=lax.Precision.HIGHEST), 'band')  33.5 us
    ppermute x8, waiting for transfers between devices, extended(): lax.ppermute(lax.slice_in_dim(block, block.shape[dim] - width, None, axis...  11 us
    ppermute x8, starting transfers between devices, extended(): lax.ppermute(lax.slice_in_dim(block, 0, width, axis=dim), axis, backward)  10.3 us
    reduce_sum x4, other arithmetic, gather_and_add(): summed = parts.sum(axis=0)  6.01 us
  transfers between devices with their start and end apart: 20, of which 18 were waited for; matrix products, arithmetic and copies ran while one was open for 3% of the time, Pallas kernels for 0%

profile of v1, /device:TPU:0, one launch (start us, length us, event | category | flops | bytes accessed | tf_op | source)
XLA Modules:
  0.0 286.6 jit_solution(21368821735371907)
XLA Ops:
  7.2 1.9 fusion.110
  9.1 1.3 collective-permute-start
  10.4 5.6 %collective-permute-start.1 = (f32[4,3,1,1440]{3,2,1,0:T(1,128)}, f32[4,3,1,1440]{3,2,1,0:T(1,128)S(1)}, u32[]{:S(2)}, u32[]{:S(2)}) collective-permute-start(f32[4,3,1,1440]{3,2,1,0:T(1,128)} %get-tuple-element.203), channel_id=1, source_target_pairs={{0,1},{1,2},{2,3},{4,5},{5,6},{6,7},{8,9},{9,10},{10,11},{12,13},{... | collective-permute-start | bytes 207368 | tf_op jit(solution)/shard_map/ppermute | solution.py:25
  16.0 2.0 fusion.108
  18.1 3.1 %sine_multiply_fusion = (f32[128,1440]{0,1:T(8,128)S(1)}, f32[128,1440]{0,1:T(8,128)S(1)}) fusion(f32[128]{0:T(128)S(1)} %compare_select_fusion), kind=kLoop, calls=%fused_computation.23 | loop fusion | flops 2027520 | bytes 1475072 | tf_op jit(solution)/shard_map/mul | solution.py:71
  23.9 1.6 broadcast_multiply_fusion.15
  26.0 1.3 collective-permute-start.2
  27.3 4.6 %collective-permute-start.3 = (f32[4,3,1,1440]{3,2,1,0:T(1,128)S(1)}, f32[4,3,1,1440]{3,2,1,0:T(1,128)S(1)}, u32[]{:S(2)}, u32[]{:S(2)}) collective-permute-start(f32[4,3,1,1440]{3,2,1,0:T(1,128)S(1)} %get-tuple-element.197), channel_id=1, source_target_pairs={{0,1},{1,2},{2,3},{4,5},{5,6},{6,7},{8,9},{9,10},{10,11},{12,13},{... | collective-permute-start | bytes 207368 | tf_op jit(solution)/shard_map/ppermute | solution.py:25
  32.3 1.6 collective-permute-done.3
  34.9 1.3 collective-permute-start.4
  36.2 4.9 %collective-permute-start.5 = (f32[4,3,1,1440]{3,2,1,0:T(1,128)S(1)}, f32[4,3,1,1440]{3,2,1,0:T(1,128)S(1)}, u32[]{:S(2)}, u32[]{:S(2)}) collective-permute-start(f32[4,3,1,1440]{3,2,1,0:T(1,128)S(1)} %get-tuple-element.191), channel_id=1, source_target_pairs={{0,1},{1,2},{2,3},{4,5},{5,6},{6,7},{8,9},{9,10},{10,11},{12,13},{... | collective-permute-start | bytes 207368 | tf_op jit(solution)/shard_map/ppermute | solution.py:25
  41.5 1.6 collective-permute-done.5
  44.2 1.3 collective-permute-start.6
  45.5 4.9 %collective-permute-start.7 = (f32[4,3,1,1440]{3,2,1,0:T(1,128)S(1)}, f32[4,3,1,1440]{3,2,1,0:T(1,128)S(1)}, u32[]{:S(2)}, u32[]{:S(2)}) collective-permute-start(f32[4,3,1,1440]{3,2,1,0:T(1,128)S(1)} %get-tuple-element.185), channel_id=1, source_target_pairs={{0,1},{1,2},{2,3},{4,5},{5,6},{6,7},{8,9},{9,10},{10,11},{12,13},{... | collective-permute-start | bytes 207368 | tf_op jit(solution)/shard_map/ppermute | solution.py:25
  50.8 1.6 collective-permute-done.7
  53.6 1.3 collective-permute-start.8
  54.9 4.9 %collective-permute-start.9 = (f32[4,3,1,1440]{3,2,1,0:T(1,128)S(1)}, f32[4,3,1,1440]{3,2,1,0:T(1,128)S(1)}, u32[]{:S(2)}, u32[]{:S(2)}) collective-permute-start(f32[4,3,1,1440]{3,2,1,0:T(1,128)S(1)} %get-tuple-element.179), channel_id=1, source_target_pairs={{0,1},{1,2},{2,3},{4,5},{5,6},{6,7},{8,9},{9,10},{10,11},{12,13},{... | collective-permute-start | bytes 207368 | tf_op jit(solution)/shard_map/ppermute | solution.py:25
  60.2 1.6 collective-permute-done.9
  63.1 1.3 collective-permute-start.10
  64.4 5.1 %collective-permute-start.11 = (f32[4,3,1,1440]{3,2,1,0:T(1,128)S(1)}, f32[4,3,1,1440]{3,2,1,0:T(1,128)S(1)}, u32[]{:S(2)}, u32[]{:S(2)}) collective-permute-start(f32[4,3,1,1440]{3,2,1,0:T(1,128)S(1)} %get-tuple-element.173), channel_id=1, source_target_pairs={{0,1},{1,2},{2,3},{4,5},{5,6},{6,7},{8,9},{9,10},{10,11},{12,13},{... | collective-permute-start | bytes 207368 | tf_op jit(solution)/shard_map/ppermute | solution.py:25
  69.7 1.6 collective-permute-done.11
  72.5 1.3 collective-permute-start.12
  73.8 4.9 %collective-permute-start.13 = (f32[4,3,1,1440]{3,2,1,0:T(1,128)S(1)}, f32[4,3,1,1440]{3,2,1,0:T(1,128)S(1)}, u32[]{:S(2)}, u32[]{:S(2)}) collective-permute-start(f32[4,3,1,1440]{3,2,1,0:T(1,128)S(1)} %get-tuple-element.167), channel_id=1, source_target_pairs={{0,1},{1,2},{2,3},{4,5},{5,6},{6,7},{8,9},{9,10},{10,11},{12,13},{... | collective-permute-start | bytes 207368 | tf_op jit(solution)/shard_map/ppermute | solution.py:25
  79.1 1.6 collective-permute-done.13
  82.0 1.3 collective-permute-start.14
  83.3 4.9 %collective-permute-start.15 = (f32[4,3,1,1440]{3,2,1,0:T(1,128)S(1)}, f32[4,3,1,1440]{3,2,1,0:T(1,128)S(1)}, u32[]{:S(2)}, u32[]{:S(2)}) collective-permute-start(f32[4,3,1,1440]{3,2,1,0:T(1,128)S(1)} %get-tuple-element.161), channel_id=1, source_target_pairs={{0,1},{1,2},{2,3},{4,5},{5,6},{6,7},{8,9},{9,10},{10,11},{12,13},{... | collective-permute-start | bytes 207368 | tf_op jit(solution)/shard_map/ppermute | solution.py:25
  88.6 1.6 collective-permute-done.15
  91.4 2.6 conditional.1
  91.6 1.0 fusion.4
  92.7 1.4 fusion
  94.2 1.1 select_n.159
  98.2 18.0 %all-gather.11.cloned.1.call-done = f32[4,4,17280]{2,1,0:T(4,128)} async-done(((f32[1,4,17280]{2,1,0:T(4,128)}), f32[4,4,17280]{2,1,0:T(4,128)}) %all-gather.11.cloned.1.call-update) | async-done | bytes 1105936 | tf_op jit(solution)/shard_map/all_gather | solution.py:15
  116.3 1.5 reduce_sum.46
  117.8 1.3 fusion.112
  119.1 11.7 %psum.56 = f32[4,4]{0,1:T(4,128)S(1)} all-reduce(f32[4,4]{0,1:T(4,128)S(1)} %fusion.112), channel_id=1, replica_groups=mesh['member'=2,'vec'=4,'band'=4] {'band'}, use_global_device_ids=true, to_apply=%region_4.5 | all-reduce | flops 16 | bytes 128 | tf_op jit(solution)/shard_map/psum | solution.py:116
  133.6 1.3 fusion.113
  134.9 8.4 %psum.57 = f32[4,4]{0,1:T(4,128)S(1)} all-reduce(f32[4,4]{0,1:T(4,128)S(1)} %fusion.113), channel_id=1, replica_groups=mesh['member'=2,'vec'=4,'band'=4] {'band'}, use_global_device_ids=true, to_apply=%region_7.10 | all-reduce | flops 16 | bytes 128 | tf_op jit(solution)/shard_map/psum | solution.py:119
  143.3 0.8 fusion.10
  144.1 0.8 select_bitcast_fusion.2
  146.8 14.0 %all-gather.13.cloned.1.call-done = f32[4,4,17280]{2,1,0:T(4,128)} async-done(((f32[1,4,17280]{2,1,0:T(4,128)}), f32[4,4,17280]{2,1,0:T(4,128)}) %all-gather.13.cloned.1.call-update) | async-done | bytes 1105936 | tf_op jit(solution)/shard_map/all_gather | solution.py:15
  160.8 1.5 reduce_sum.47
  162.3 1.3 fusion.114
  163.6 11.9 %psum.58 = f32[4,4]{0,1:T(4,128)S(1)} all-reduce(f32[4,4]{0,1:T(4,128)S(1)} %fusion.114), channel_id=1, replica_groups=mesh['member'=2,'vec'=4,'band'=4] {'band'}, use_global_device_ids=true, to_apply=%region_9.12 | all-reduce | flops 16 | bytes 128 | tf_op jit(solution)/shard_map/psum | solution.py:116
  178.3 1.3 fusion.115
  179.6 8.4 %psum.59 = f32[4,4]{0,1:T(4,128)S(1)} all-reduce(f32[4,4]{0,1:T(4,128)S(1)} %fusion.115), channel_id=1, replica_groups=mesh['member'=2,'vec'=4,'band'=4] {'band'}, use_global_device_ids=true, to_apply=%region_10.13 | all-reduce | flops 16 | bytes 128 | tf_op jit(solution)/shard_map/psum | solution.py:119
  188.0 0.8 fusion.9
  188.8 0.8 select_bitcast_fusion.1
  191.5 13.9 %all-gather.15.cloned.1.call-done = f32[4,4,17280]{2,1,0:T(4,128)} async-done(((f32[1,4,17280]{2,1,0:T(4,128)}), f32[4,4,17280]{2,1,0:T(4,128)}) %all-gather.15.cloned.1.call-update) | async-done | bytes 1105936 | tf_op jit(solution)/shard_map/all_gather | solution.py:15
  205.5 1.5 reduce_sum.48
  207.0 1.3 fusion.116
  208.3 11.7 %psum.60 = f32[4,4]{0,1:T(4,128)S(1)} all-reduce(f32[4,4]{0,1:T(4,128)S(1)} %fusion.116), channel_id=1, replica_groups=mesh['member'=2,'vec'=4,'band'=4] {'band'}, use_global_device_ids=true, to_apply=%region_12.15 | all-reduce | flops 16 | bytes 128 | tf_op jit(solution)/shard_map/psum | solution.py:116
  222.1 0.7 fusion.62
  222.8 1.3 fusion.117
  224.1 8.4 %psum.61 = f32[4,4]{0,1:T(4,128)S(1)} all-reduce(f32[4,4]{0,1:T(4,128)S(1)} %fusion.117), channel_id=1, replica_groups=mesh['member'=2,'vec'=4,'band'=4] {'band'}, use_global_device_ids=true, to_apply=%region_13.16 | all-reduce | flops 16 | bytes 128 | tf_op jit(solution)/shard_map/psum | solution.py:119
  232.5 0.8 fusion.8
  233.3 0.8 select_bitcast_fusion
  237.3 12.7 %all-gather.17.cloned.1.call-done = f32[4,4,17280]{2,1,0:T(4,128)} async-done(((f32[1,4,17280]{2,1,0:T(4,128)}), f32[4,4,17280]{2,1,0:T(4,128)}) %all-gather.17.cloned.1.call-update) | async-done | bytes 1105936 | tf_op jit(solution)/shard_map/all_gather | solution.py:15
  250.0 1.5 reduce_sum.49
  251.5 1.3 fusion.118
  252.8 11.7 %psum.62 = f32[4,4]{0,1:T(4,128)S(1)} all-reduce(f32[4,4]{0,1:T(4,128)S(1)} %fusion.118), channel_id=1, replica_groups=mesh['member'=2,'vec'=4,'band'=4] {'band'}, use_global_device_ids=true, to_apply=%region_15.18 | all-reduce | flops 16 | bytes 128 | tf_op jit(solution)/shard_map/psum | solution.py:116
  268.0 1.3 fusion.119
  269.3 8.4 %psum.63 = f32[4,4]{0,1:T(4,128)S(1)} all-reduce(f32[4,4]{0,1:T(4,128)S(1)} %fusion.119), channel_id=1, replica_groups=mesh['member'=2,'vec'=4,'band'=4] {'band'}, use_global_device_ids=true, to_apply=%region_16.19 | all-reduce | flops 16 | bytes 128 | tf_op jit(solution)/shard_map/psum | solution.py:119
  277.6 0.8 fusion.7
  278.5 1.1 reshape.87
  (126 shorter events, 28.9 us)
Async XLA Ops:
  7.2 10.8 %copy-start = (f32[4,3,4,1440]{3,2,1,0:T(4,128)S(1)}, f32[4,3,4,1440]{3,2,1,0:T(4,128)}, u32[]{:S(2)}) copy-start(f32[4,3,4,1440]{3,2,1,0:T(4,128)} %param.9) | copy-start | bytes 829444
  7.2 10.9 %copy-start.1 = (f32[4,4,1440]{2,1,0:T(4,128)S(1)}, f32[4,4,1440]{2,1,0:T(4,128)}, u32[]{:S(2)}) copy-start(f32[4,4,1440]{2,1,0:T(4,128)} %param.10) | copy-start | bytes 276484
  7.2 109.1 %all-gather.11.cloned.1.call-start = ((), (), s32[]{:S(2)}) async-start(), calls=%async_computation | async-start | bytes 1382400 | tf_op jit(solution)/shard_map/all_gather | solution.py:15
  9.1 14.1 %collective-permute-start = (f32[4,3,1,1440]{3,2,1,0:T(1,128)}, f32[4,3,1,1440]{3,2,1,0:T(1,128)S(1)}, u32[]{:S(2)}, u32[]{:S(2)}) collective-permute-start(f32[4,3,1,1440]{3,2,1,0:T(1,128)} %get-tuple-element.202), channel_id=1, source_target_pairs={{1,0},{2,1},{3,2},{5,4},{6,5},{7,6},{9,8},{10,9},{11,10},{13,12},{... | collective-permute-start | bytes 207368 | tf_op jit(solution)/shard_map/ppermute | solution.py:28
  10.4 12.8 %collective-permute-start.1 = (f32[4,3,1,1440]{3,2,1,0:T(1,128)}, f32[4,3,1,1440]{3,2,1,0:T(1,128)S(1)}, u32[]{:S(2)}, u32[]{:S(2)}) collective-permute-start(f32[4,3,1,1440]{3,2,1,0:T(1,128)} %get-tuple-element.203), channel_id=1, source_target_pairs={{0,1},{1,2},{2,3},{4,5},{5,6},{6,7},{8,9},{9,10},{10,11},{12,13},{... | collective-permute-start | bytes 207368 | tf_op jit(solution)/shard_map/ppermute | solution.py:25
  21.2 0.7 copy-start.4
  23.2 0.6 copy-start.2
  23.2 0.7 copy-start.3
  26.0 6.2 %collective-permute-start.2 = (f32[4,3,1,1440]{3,2,1,0:T(1,128)S(1)}, f32[4,3,1,1440]{3,2,1,0:T(1,128)S(1)}, u32[]{:S(2)}, u32[]{:S(2)}) collective-permute-start(f32[4,3,1,1440]{3,2,1,0:T(1,128)S(1)} %get-tuple-element.196), channel_id=1, source_target_pairs={{1,0},{2,1},{3,2},{5,4},{6,5},{7,6},{9,8},{10,9},{11,10},{13,12},{... | collective-permute-start | bytes 207368 | tf_op jit(solution)/shard_map/ppermute | solution.py:28
  27.3 6.5 %collective-permute-start.3 = (f32[4,3,1,1440]{3,2,1,0:T(1,128)S(1)}, f32[4,3,1,1440]{3,2,1,0:T(1,128)S(1)}, u32[]{:S(2)}, u32[]{:S(2)}) collective-permute-start(f32[4,3,1,1440]{3,2,1,0:T(1,128)S(1)} %get-tuple-element.197), channel_id=1, source_target_pairs={{0,1},{1,2},{2,3},{4,5},{5,6},{6,7},{8,9},{9,10},{10,11},{12,13},{... | collective-permute-start | bytes 207368 | tf_op jit(solution)/shard_map/ppermute | solution.py:25
  34.9 6.6 %collective-permute-start.4 = (f32[4,3,1,1440]{3,2,1,0:T(1,128)S(1)}, f32[4,3,1,1440]{3,2,1,0:T(1,128)S(1)}, u32[]{:S(2)}, u32[]{:S(2)}) collective-permute-start(f32[4,3,1,1440]{3,2,1,0:T(1,128)S(1)} %get-tuple-element.190), channel_id=1, source_target_pairs={{1,0},{2,1},{3,2},{5,4},{6,5},{7,6},{9,8},{10,9},{11,10},{13,12},{... | collective-permute-start | bytes 207368 | tf_op jit(solution)/shard_map/ppermute | solution.py:28
  36.2 6.9 %collective-permute-start.5 = (f32[4,3,1,1440]{3,2,1,0:T(1,128)S(1)}, f32[4,3,1,1440]{3,2,1,0:T(1,128)S(1)}, u32[]{:S(2)}, u32[]{:S(2)}) collective-permute-start(f32[4,3,1,1440]{3,2,1,0:T(1,128)S(1)} %get-tuple-element.191), channel_id=1, source_target_pairs={{0,1},{1,2},{2,3},{4,5},{5,6},{6,7},{8,9},{9,10},{10,11},{12,13},{... | collective-permute-start | bytes 207368 | tf_op jit(solution)/shard_map/ppermute | solution.py:25
  44.2 6.6 %collective-permute-start.6 = (f32[4,3,1,1440]{3,2,1,0:T(1,128)S(1)}, f32[4,3,1,1440]{3,2,1,0:T(1,128)S(1)}, u32[]{:S(2)}, u32[]{:S(2)}) collective-permute-start(f32[4,3,1,1440]{3,2,1,0:T(1,128)S(1)} %get-tuple-element.184), channel_id=1, source_target_pairs={{1,0},{2,1},{3,2},{5,4},{6,5},{7,6},{9,8},{10,9},{11,10},{13,12},{... | collective-permute-start | bytes 207368 | tf_op jit(solution)/shard_map/ppermute | solution.py:28
  45.5 6.9 %collective-permute-start.7 = (f32[4,3,1,1440]{3,2,1,0:T(1,128)S(1)}, f32[4,3,1,1440]{3,2,1,0:T(1,128)S(1)}, u32[]{:S(2)}, u32[]{:S(2)}) collective-permute-start(f32[4,3,1,1440]{3,2,1,0:T(1,128)S(1)} %get-tuple-element.185), channel_id=1, source_target_pairs={{0,1},{1,2},{2,3},{4,5},{5,6},{6,7},{8,9},{9,10},{10,11},{12,13},{... | collective-permute-start | bytes 207368 | tf_op jit(solution)/shard_map/ppermute | solution.py:25
  53.6 6.6 %collective-permute-start.8 = (f32[4,3,1,1440]{3,2,1,0:T(1,128)S(1)}, f32[4,3,1,1440]{3,2,1,0:T(1,128)S(1)}, u32[]{:S(2)}, u32[]{:S(2)}) collective-permute-start(f32[4,3,1,1440]{3,2,1,0:T(1,128)S(1)} %get-tuple-element.178), channel_id=1, source_target_pairs={{1,0},{2,1},{3,2},{5,4},{6,5},{7,6},{9,8},{10,9},{11,10},{13,12},{... | collective-permute-start | bytes 207368 | tf_op jit(solution)/shard_map/ppermute | solution.py:28
  54.9 6.9 %collective-permute-start.9 = (f32[4,3,1,1440]{3,2,1,0:T(1,128)S(1)}, f32[4,3,1,1440]{3,2,1,0:T(1,128)S(1)}, u32[]{:S(2)}, u32[]{:S(2)}) collective-permute-start(f32[4,3,1,1440]{3,2,1,0:T(1,128)S(1)} %get-tuple-element.179), channel_id=1, source_target_pairs={{0,1},{1,2},{2,3},{4,5},{5,6},{6,7},{8,9},{9,10},{10,11},{12,13},{... | collective-permute-start | bytes 207368 | tf_op jit(solution)/shard_map/ppermute | solution.py:25
  63.1 6.6 %collective-permute-start.10 = (f32[4,3,1,1440]{3,2,1,0:T(1,128)S(1)}, f32[4,3,1,1440]{3,2,1,0:T(1,128)S(1)}, u32[]{:S(2)}, u32[]{:S(2)}) collective-permute-start(f32[4,3,1,1440]{3,2,1,0:T(1,128)S(1)} %get-tuple-element.172), channel_id=1, source_target_pairs={{1,0},{2,1},{3,2},{5,4},{6,5},{7,6},{9,8},{10,9},{11,10},{13,12},{... | collective-permute-start | bytes 207368 | tf_op jit(solution)/shard_map/ppermute | solution.py:28
  64.4 6.9 %collective-permute-start.11 = (f32[4,3,1,1440]{3,2,1,0:T(1,128)S(1)}, f32[4,3,1,1440]{3,2,1,0:T(1,128)S(1)}, u32[]{:S(2)}, u32[]{:S(2)}) collective-permute-start(f32[4,3,1,1440]{3,2,1,0:T(1,128)S(1)} %get-tuple-element.173), channel_id=1, source_target_pairs={{0,1},{1,2},{2,3},{4,5},{5,6},{6,7},{8,9},{9,10},{10,11},{12,13},{... | collective-permute-start | bytes 207368 | tf_op jit(solution)/shard_map/ppermute | solution.py:25
  72.5 6.6 %collective-permute-start.12 = (f32[4,3,1,1440]{3,2,1,0:T(1,128)S(1)}, f32[4,3,1,1440]{3,2,1,0:T(1,128)S(1)}, u32[]{:S(2)}, u32[]{:S(2)}) collective-permute-start(f32[4,3,1,1440]{3,2,1,0:T(1,128)S(1)} %get-tuple-element.166), channel_id=1, source_target_pairs={{1,0},{2,1},{3,2},{5,4},{6,5},{7,6},{9,8},{10,9},{11,10},{13,12},{... | collective-permute-start | bytes 207368 | tf_op jit(solution)/shard_map/ppermute | solution.py:28
  73.8 6.9 %collective-permute-start.13 = (f32[4,3,1,1440]{3,2,1,0:T(1,128)S(1)}, f32[4,3,1,1440]{3,2,1,0:T(1,128)S(1)}, u32[]{:S(2)}, u32[]{:S(2)}) collective-permute-start(f32[4,3,1,1440]{3,2,1,0:T(1,128)S(1)} %get-tuple-element.167), channel_id=1, source_target_pairs={{0,1},{1,2},{2,3},{4,5},{5,6},{6,7},{8,9},{9,10},{10,11},{12,13},{... | collective-permute-start | bytes 207368 | tf_op jit(solution)/shard_map/ppermute | solution.py:25
  82.0 6.6 %collective-permute-start.14 = (f32[4,3,1,1440]{3,2,1,0:T(1,128)S(1)}, f32[4,3,1,1440]{3,2,1,0:T(1,128)S(1)}, u32[]{:S(2)}, u32[]{:S(2)}) collective-permute-start(f32[4,3,1,1440]{3,2,1,0:T(1,128)S(1)} %get-tuple-element.160), channel_id=1, source_target_pairs={{1,0},{2,1},{3,2},{5,4},{6,5},{7,6},{9,8},{10,9},{11,10},{13,12},{... | collective-permute-start | bytes 207368 | tf_op jit(solution)/shard_map/ppermute | solution.py:28
  83.3 6.9 %collective-permute-start.15 = (f32[4,3,1,1440]{3,2,1,0:T(1,128)S(1)}, f32[4,3,1,1440]{3,2,1,0:T(1,128)S(1)}, u32[]{:S(2)}, u32[]{:S(2)}) collective-permute-start(f32[4,3,1,1440]{3,2,1,0:T(1,128)S(1)} %get-tuple-element.161), channel_id=1, source_target_pairs={{0,1},{1,2},{2,3},{4,5},{5,6},{6,7},{8,9},{9,10},{10,11},{12,13},{... | collective-permute-start | bytes 207368 | tf_op jit(solution)/shard_map/ppermute | solution.py:25
  90.8 0.7 copy-start.5
  95.3 65.5 %all-gather.13.cloned.1.call-start = ((), (), s32[]{:S(2)}) async-start(), calls=%async_computation.1 | async-start | bytes 1382400 | tf_op jit(solution)/shard_map/all_gather | solution.py:15
  144.9 60.6 %all-gather.15.cloned.1.call-start = ((), (), s32[]{:S(2)}) async-start(), calls=%async_computation.2 | async-start | bytes 1382400 | tf_op jit(solution)/shard_map/all_gather | solution.py:15
  189.6 60.4 %all-gather.17.cloned.1.call-start = ((), (), s32[]{:S(2)}) async-start(), calls=%async_computation.3 | async-start | bytes 1382400 | tf_op jit(solution)/shard_map/all_gather | solution.py:15
Sparse Core Ops, SparseCore 0:
  95.4 20.8 all-gather.10
  145.0 15.7 all-gather.12
  189.7 15.7 all-gather.14
  234.2 15.7 all-gather.16
